TPU v7x, 32 devices: a whole 2x2x4 slice. The times are simulated.
32 devices in a mesh: ctx: 8 (over y, x, core), fsdp: 4 (over z).
Axes of the slice: x: 2, y: 2, z: 4, core: 2. Of those that a mesh axis runs over, the one named last changes fastest.
Arguments:
- layer_in: bfloat16 [8, 1024, 1024], P('fsdp', 'ctx'), may hold values from -6 to 6
- block_order: int32 [8, 16], P('fsdp'), may hold values from 0 to 15, as said below
- ln1_gain: bfloat16 [1024], P('fsdp'), may hold values from 0.5 to 1.5
- ln1_shift: bfloat16 [1024], P('fsdp'), may hold values from -3 to 3
- w_qkv: bfloat16 [1024, 3072], P('fsdp'), may hold values from -0.1875 to 0.1875
- b_query: bfloat16 [1024], P('fsdp'), may hold values from -3 to 3
- b_value: bfloat16 [1024], P('fsdp'), may hold values from -3 to 3
- w_out: bfloat16 [1024, 1024], P('fsdp'), may hold values from -1 to 1
- b_out: bfloat16 [1024], P('fsdp'), may hold values from -2 to 2
- ln2_gain: bfloat16 [1024], P('fsdp'), may hold values from 0.5 to 1.5
- ln2_shift: bfloat16 [1024], P('fsdp'), may hold values from -3 to 3
- w_up: bfloat16 [1024, 4096], P('fsdp'), may hold values from -0.1875 to 0.1875
- b_up: bfloat16 [4096], P('fsdp'), may hold values from -3 to 3
- w_down: bfloat16 [4096, 1024], P('fsdp'), may hold values from -0.09375 to 0.09375
- b_down: bfloat16 [1024], P('fsdp'), may hold values from -3 to 3
- cotangent: bfloat16 [8, 1024, 1024], P('fsdp', 'ctx'), may hold values from -6 to 6
Outputs:
- layer_out: bfloat16 [8, 1024, 1024], P('fsdp', 'ctx')
- input_grad: bfloat16 [8, 1024, 1024], P('fsdp', 'ctx')
- grad_ln1_gain: float32 [1024], P(('ctx', 'fsdp'))
- grad_ln1_shift: float32 [1024], P(('ctx', 'fsdp'))
- grad_w_qkv: float32 [1024, 3072], P(('ctx', 'fsdp'))
- grad_b_query: float32 [1024], P(('ctx', 'fsdp'))
- grad_b_value: float32 [1024], P(('ctx', 'fsdp'))
- grad_w_out: float32 [1024, 1024], P(('ctx', 'fsdp'))
- grad_b_out: float32 [1024], P(('ctx', 'fsdp'))
- grad_ln2_gain: float32 [1024], P(('ctx', 'fsdp'))
- grad_ln2_shift: float32 [1024], P(('ctx', 'fsdp'))
- grad_w_up: float32 [1024, 4096], P(('ctx', 'fsdp'))
- grad_b_up: float32 [4096], P(('ctx', 'fsdp'))
- grad_w_down: float32 [4096, 1024], P(('ctx', 'fsdp'))
- grad_b_down: float32 [1024], P(('ctx', 'fsdp'))
Inputs may be any that keep to these rules, and one draw needn't show every extreme that they name: Stored block j of sequence s (rows j * 64 to (j + 1) * 64 - 1 as stored) holds block block_order[s, j] of the true order; each row is a permutation, and entry 2c + 1 is 15 minus entry 2c.
All inputs are finite; a program needn't handle non-finite values.
Results may differ from a plain program's by a relative error of at most 0.012.
Values may be sent and summed in bfloat16 or wider, within the bound.
A program may use at most 512 MiB of HBM per device.

v0:
```python
import math
import jax
import jax.numpy as jnp
from jax import lax
from jax.sharding import PartitionSpec as P

D = 1024
HEADS = 8
HEAD_DIM = 128
EPSILON = 1e-05
NEG_LARGE = -1e30
GELU_C = math.sqrt(2.0 / math.pi)
GELU_K = 0.044715


def gelu_tanh(values):
    inner = jnp.tanh(GELU_C * (values + GELU_K * values * values * values))
    return 0.5 * values * (1.0 + inner)


def gelu_slope(values):
    inner = jnp.tanh(GELU_C * (values + GELU_K * values * values * values))
    return 0.5 * (1.0 + inner) + 0.5 * values * (1.0 - inner * inner) * GELU_C * (
        1.0 + 3.0 * GELU_K * values * values
    )


def normalize(values, gain_vec, shift_vec):
    average = jnp.mean(values, axis=-1, keepdims=True)
    centered = values - average
    inv_dev = lax.rsqrt(jnp.mean(centered * centered, axis=-1, keepdims=True) + EPSILON)
    normed = centered * inv_dev
    return (normed * gain_vec + shift_vec, normed, inv_dev)


def normalize_back(grad, normed, inv_dev, gain_vec):
    scaled = grad * gain_vec
    return inv_dev * (
        scaled
        - jnp.mean(scaled, axis=-1, keepdims=True)
        - normed * jnp.mean(scaled * normed, axis=-1, keepdims=True)
    )


def token_positions(order_row, seq_len, half_rows):
    rows = jnp.arange(seq_len, dtype=jnp.int32)
    slots = jnp.arange(order_row.shape[0], dtype=jnp.int32)
    picked = jnp.sum(
        jnp.where((rows // half_rows)[:, None] == slots[None, :], order_row[None, :], 0), axis=1
    )
    return picked * half_rows + rows % half_rows


def block_probs(query_heads, key_heads, query_pos, key_pos, row_lse, scale):
    raw_scores = jnp.einsum(
        "qhd,khd->hqk", query_heads, key_heads, preferred_element_type=jnp.float32
    )
    allowed = (query_pos[:, None] >= key_pos[None, :])[None]
    shifted = jnp.where(allowed, raw_scores * scale - row_lse[:, :, None], NEG_LARGE)
    return jnp.where(allowed, jnp.exp(shifted), 0.0)


def score_grads(probs, grad_probs, row_delta, scale):
    return (probs * (grad_probs - row_delta[:, :, None]) * scale).astype(jnp.bfloat16)


def per_device(
    layer_in,
    block_order,
    ln1_gain,
    ln1_shift,
    w_qkv,
    b_query,
    b_value,
    w_out,
    b_out,
    ln2_gain,
    ln2_shift,
    w_up,
    b_up,
    w_down,
    b_down,
    cotangent,
):
    full = (
        lax.all_gather(ln1_gain, "fsdp", axis=0, tiled=True),
        lax.all_gather(ln1_shift, "fsdp", axis=0, tiled=True),
        lax.all_gather(w_qkv, "fsdp", axis=0, tiled=True),
        lax.all_gather(b_query, "fsdp", axis=0, tiled=True),
        lax.all_gather(b_value, "fsdp", axis=0, tiled=True),
        lax.all_gather(w_out, "fsdp", axis=0, tiled=True),
        lax.all_gather(b_out, "fsdp", axis=0, tiled=True),
        lax.all_gather(ln2_gain, "fsdp", axis=0, tiled=True),
        lax.all_gather(ln2_shift, "fsdp", axis=0, tiled=True),
        lax.all_gather(w_up, "fsdp", axis=0, tiled=True),
        lax.all_gather(b_up, "fsdp", axis=0, tiled=True),
        lax.all_gather(w_down, "fsdp", axis=0, tiled=True),
        lax.all_gather(b_down, "fsdp", axis=0, tiled=True),
    )
    qkv_full, out_full, up_full, down_full = (full[2], full[5], full[9], full[11])
    first_gain = full[0].astype(jnp.float32)
    first_shift = full[1].astype(jnp.float32)
    query_bias = full[3].astype(jnp.float32)
    value_bias = full[4].astype(jnp.float32)
    out_bias = full[6].astype(jnp.float32)
    second_gain = full[7].astype(jnp.float32)
    second_shift = full[8].astype(jnp.float32)
    up_bias = full[10].astype(jnp.float32)
    down_bias = full[12].astype(jnp.float32)
    micro = layer_in.shape[0]
    tokens = layer_in.shape[1]
    seq_len = tokens * lax.axis_size("ctx")
    half_rows = tokens // 2
    key_block = min(512, seq_len)
    blocks = seq_len // key_block
    scale = HEAD_DIM ** (-0.5)
    here = lax.axis_index("ctx")
    heads_shape = (blocks, key_block, HEADS, HEAD_DIM)
    totals = [jnp.zeros(item.shape, jnp.float32) for item in full]
    outputs_fwd = []
    outputs_grad = []
    for micro_step in range(micro):
        pos_all = token_positions(block_order[micro_step], seq_len, half_rows)
        pos_mine = lax.dynamic_slice_in_dim(pos_all, here * tokens, tokens)
        pos_blocks = pos_all.reshape(blocks, key_block)
        inputs = layer_in[micro_step].astype(jnp.float32)
        first_out, first_normed, first_inv = normalize(inputs, first_gain, first_shift)
        first_low = first_out.astype(jnp.bfloat16)
        projected = jnp.dot(first_low, qkv_full, preferred_element_type=jnp.float32)
        query_low = (projected[:, :D] + query_bias).astype(jnp.bfloat16)
        key_low = projected[:, D : 2 * D].astype(jnp.bfloat16)
        value_low = (projected[:, 2 * D :] + value_bias).astype(jnp.bfloat16)
        keys_all, values_all = (
            lax.all_gather(key_low, "ctx", axis=0, tiled=True),
            lax.all_gather(value_low, "ctx", axis=0, tiled=True),
        )
        query_heads = query_low.reshape(tokens, HEADS, HEAD_DIM)
        key_blocks = keys_all.reshape(heads_shape)
        value_blocks = values_all.reshape(heads_shape)

        def stats_step(carry, piece):
            run_max, run_sum = carry
            key_piece, key_pos = piece
            raw_scores = (
                jnp.einsum(
                    "qhd,khd->hqk", query_heads, key_piece, preferred_element_type=jnp.float32
                )
                * scale
            )
            allowed = (pos_mine[:, None] >= key_pos[None, :])[None]
            masked = jnp.where(allowed, raw_scores, NEG_LARGE)
            new_max = jnp.maximum(run_max, jnp.max(masked, axis=-1))
            weights = jnp.where(allowed, jnp.exp(masked - new_max[:, :, None]), 0.0)
            run_sum = run_sum * jnp.exp(run_max - new_max) + jnp.sum(weights, axis=-1)
            return ((new_max, run_sum), None)

        start_state = (
            jnp.full((HEADS, tokens), NEG_LARGE, jnp.float32),
            jnp.zeros((HEADS, tokens), jnp.float32),
        )
        (run_max, run_sum), unused = lax.scan(stats_step, start_state, (key_blocks, pos_blocks))
        row_lse = run_max + jnp.log(run_sum)

        def output_step(carry, piece):
            acc_low, acc_exact = carry
            key_piece, value_piece, key_pos = piece
            probs = block_probs(query_heads, key_piece, pos_mine, key_pos, row_lse, scale)
            acc_low = acc_low + jnp.einsum(
                "hqk,khd->hqd",
                probs.astype(jnp.bfloat16),
                value_piece,
                preferred_element_type=jnp.float32,
            )
            acc_exact = acc_exact + jnp.einsum(
                "hqk,khd->hqd",
                probs,
                value_piece.astype(jnp.float32),
                preferred_element_type=jnp.float32,
            )
            return ((acc_low, acc_exact), None)

        start_acc = (
            jnp.zeros((HEADS, tokens, HEAD_DIM), jnp.float32),
            jnp.zeros((HEADS, tokens, HEAD_DIM), jnp.float32),
        )
        (attn_heads, exact_heads), unused = lax.scan(
            output_step, start_acc, (key_blocks, value_blocks, pos_blocks)
        )
        attn_low = jnp.transpose(attn_heads, (1, 0, 2)).reshape(tokens, D).astype(jnp.bfloat16)
        resid = inputs + jnp.dot(attn_low, out_full, preferred_element_type=jnp.float32) + out_bias
        second_out, second_normed, second_inv = normalize(resid, second_gain, second_shift)
        second_low = second_out.astype(jnp.bfloat16)
        hidden = jnp.dot(second_low, up_full, preferred_element_type=jnp.float32) + up_bias
        active_low = gelu_tanh(hidden).astype(jnp.bfloat16)
        result = (
            resid + jnp.dot(active_low, down_full, preferred_element_type=jnp.float32) + down_bias
        )
        outputs_fwd.append(result.astype(jnp.bfloat16))
        grad_out = cotangent[micro_step]
        grad_outf = grad_out.astype(jnp.float32)
        term_down = jnp.einsum(
            "tf,td->fd", active_low, grad_out, preferred_element_type=jnp.float32
        )
        grad_active = jnp.einsum(
            "td,fd->tf", grad_out, down_full, preferred_element_type=jnp.float32
        )
        grad_hidden = (grad_active * gelu_slope(hidden)).astype(jnp.bfloat16)
        term_up = jnp.einsum(
            "td,tf->df", second_low, grad_hidden, preferred_element_type=jnp.float32
        )
        grad_second = jnp.einsum(
            "tf,df->td", grad_hidden, up_full, preferred_element_type=jnp.float32
        )
        grad_resid = grad_outf + normalize_back(grad_second, second_normed, second_inv, second_gain)
        grad_branch = grad_resid.astype(jnp.bfloat16)
        term_out = jnp.einsum(
            "td,te->de", attn_low, grad_branch, preferred_element_type=jnp.float32
        )
        grad_attn = jnp.einsum(
            "te,de->td", grad_branch, out_full, preferred_element_type=jnp.float32
        ).astype(jnp.bfloat16)
        grad_heads = grad_attn.reshape(tokens, HEADS, HEAD_DIM)
        row_delta = jnp.einsum("qhd,hqd->hq", grad_heads.astype(jnp.float32), exact_heads)

        def backward_step(grad_query, piece):
            key_piece, value_piece, key_pos = piece
            probs = block_probs(query_heads, key_piece, pos_mine, key_pos, row_lse, scale)
            grad_value = jnp.einsum(
                "hqk,qhd->khd",
                probs.astype(jnp.bfloat16),
                grad_heads,
                preferred_element_type=jnp.float32,
            )
            grad_probs = jnp.einsum(
                "qhd,khd->hqk", grad_heads, value_piece, preferred_element_type=jnp.float32
            )
            grad_scores = score_grads(probs, grad_probs, row_delta, scale)
            grad_query = grad_query + jnp.einsum(
                "hqk,khd->qhd", grad_scores, key_piece, preferred_element_type=jnp.float32
            )
            grad_key = jnp.einsum(
                "hqk,qhd->khd", grad_scores, query_heads, preferred_element_type=jnp.float32
            )
            rows_here = key_piece.shape[0]
            return (
                grad_query,
                jnp.concatenate(
                    [grad_key.reshape(rows_here, D), grad_value.reshape(rows_here, D)], axis=1
                ),
            )

        grad_query, key_terms = lax.scan(
            backward_step,
            jnp.zeros((tokens, HEADS, HEAD_DIM), jnp.float32),
            (key_blocks, value_blocks, pos_blocks),
        )
        key_sums = lax.psum_scatter(
            key_terms.reshape(seq_len, 2 * D), "ctx", scatter_dimension=0, tiled=True
        )
        grad_key_low = key_sums[:, :D].astype(jnp.bfloat16)
        grad_value_low = key_sums[:, D:].astype(jnp.bfloat16)
        grad_query_low = grad_query.reshape(tokens, D).astype(jnp.bfloat16)
        grad_projected = jnp.concatenate([grad_query_low, grad_key_low, grad_value_low], axis=1)
        term_qkv = jnp.einsum(
            "td,te->de", first_low, grad_projected, preferred_element_type=jnp.float32
        )
        grad_first = jnp.einsum(
            "te,de->td", grad_projected, qkv_full, preferred_element_type=jnp.float32
        )
        grad_input = grad_resid + normalize_back(grad_first, first_normed, first_inv, first_gain)
        outputs_grad.append(grad_input.astype(jnp.bfloat16))
        terms = (
            jnp.sum(grad_first * first_normed, axis=0),
            jnp.sum(grad_first, axis=0),
            term_qkv,
            jnp.sum(grad_query_low.astype(jnp.float32), axis=0),
            jnp.sum(grad_value_low.astype(jnp.float32), axis=0),
            term_out,
            jnp.sum(grad_branch.astype(jnp.float32), axis=0),
            jnp.sum(grad_second * second_normed, axis=0),
            jnp.sum(grad_second, axis=0),
            term_up,
            jnp.sum(grad_hidden.astype(jnp.float32), axis=0),
            term_down,
            jnp.sum(grad_outf, axis=0),
        )
        totals = [older + newer for older, newer in zip(totals, terms)]
    summed = (
        lax.psum_scatter(totals[0], ("ctx", "fsdp"), scatter_dimension=0, tiled=True),
        lax.psum_scatter(totals[1], ("ctx", "fsdp"), scatter_dimension=0, tiled=True),
        lax.psum_scatter(totals[2], ("ctx", "fsdp"), scatter_dimension=0, tiled=True),
        lax.psum_scatter(totals[3], ("ctx", "fsdp"), scatter_dimension=0, tiled=True),
        lax.psum_scatter(totals[4], ("ctx", "fsdp"), scatter_dimension=0, tiled=True),
        lax.psum_scatter(totals[5], ("ctx", "fsdp"), scatter_dimension=0, tiled=True),
        lax.psum_scatter(totals[6], ("ctx", "fsdp"), scatter_dimension=0, tiled=True),
        lax.psum_scatter(totals[7], ("ctx", "fsdp"), scatter_dimension=0, tiled=True),
        lax.psum_scatter(totals[8], ("ctx", "fsdp"), scatter_dimension=0, tiled=True),
        lax.psum_scatter(totals[9], ("ctx", "fsdp"), scatter_dimension=0, tiled=True),
        lax.psum_scatter(totals[10], ("ctx", "fsdp"), scatter_dimension=0, tiled=True),
        lax.psum_scatter(totals[11], ("ctx", "fsdp"), scatter_dimension=0, tiled=True),
        lax.psum_scatter(totals[12], ("ctx", "fsdp"), scatter_dimension=0, tiled=True),
    )
    return (
        jnp.stack(outputs_fwd),
        jnp.stack(outputs_grad),
        summed[0],
        summed[1],
        summed[2],
        summed[3],
        summed[4],
        summed[5],
        summed[6],
        summed[7],
        summed[8],
        summed[9],
        summed[10],
        summed[11],
        summed[12],
    )


def solution(mesh):
    placed = (
        P("fsdp", "ctx", None),
        P("fsdp", None),
        P("fsdp"),
        P("fsdp"),
        P("fsdp", None),
        P("fsdp"),
        P("fsdp"),
        P("fsdp", None),
        P("fsdp"),
        P("fsdp"),
        P("fsdp"),
        P("fsdp", None),
        P("fsdp"),
        P("fsdp", None),
        P("fsdp"),
        P("fsdp", "ctx", None),
    )
    return jax.shard_map(
        per_device,
        mesh=mesh,
        in_specs=placed,
        out_specs=(
            P("fsdp", "ctx", None),
            P("fsdp", "ctx", None),
            P(("ctx", "fsdp")),
            P(("ctx", "fsdp")),
            P(("ctx", "fsdp"), None),
            P(("ctx", "fsdp")),
            P(("ctx", "fsdp")),
            P(("ctx", "fsdp"), None),
            P(("ctx", "fsdp")),
            P(("ctx", "fsdp")),
            P(("ctx", "fsdp")),
            P(("ctx", "fsdp"), None),
            P(("ctx", "fsdp")),
            P(("ctx", "fsdp"), None),
            P(("ctx", "fsdp")),
        ),
        check_vma=False,
    )
```

profile of v0, /device:TPU:0, one launch (start us, length us, event | category | flops | bytes accessed | tf_op | source)
XLA Modules:
  0.0 1857.9 jit_solution(17294477554371182860)
XLA Ops:
  9.3 12.6 all-gather.1
  21.9 7.8 all-gather
  31.3 96.4 %all-gather.17.cloned.1.call-done = bf16[1024,3072]{1,0:T(8,128)(2,1)} async-done(((bf16[256,3072]{1,0:T(8,128)(2,1)}), bf16[1024,3072]{1,0:T(8,128)(2,1)}) %all-gather.17.cloned.1.call-update) | async-done | bytes 6291472 | tf_op jit(solution)/shard_map/all_gather | solution.py:88
  127.7 3.9 fusion.169
  132.4 7.9 all-gather.3
  140.4 9.2 all-gather.2
  149.6 3.9 fusion.166
  159.8 8.3 all-gather.6
  168.1 8.9 all-gather.5
  176.9 8.3 all-gather.4
  185.2 12.0 all_gather.63
  199.4 2.2 copy.257
  203.3 2.2 copy.258
  207.3 11.5 all-gather.21.cloned.1.call-done
  221.4 27.1 %all-gather.19.cloned.1.call-done = bf16[1024,1024]{1,0:T(8,128)(2,1)} async-done(((bf16[128,1024]{1,0:T(8,128)(2,1)}), bf16[1024,1024]{1,0:T(8,128)(2,1)}) %all-gather.19.cloned.1.call-update) | async-done | bytes 2097168 | tf_op jit(solution)/shard_map/all_gather | solution.py:134
  252.4 5.0 while.80
  257.4 10.1 while.81
  257.6 2.3 fusion.290
  269.4 4.9 while.78
  274.2 7.6 while.79
  282.7 13.1 all-gather.23.cloned.1.call-done
  295.8 2.4 fusion.173
  299.8 146.0 %all-gather.25.cloned.1.call-done = bf16[1024,4096]{1,0:T(8,128)(2,1)} async-done(((bf16[256,4096]{1,0:T(8,128)(2,1)}), bf16[1024,4096]{1,0:T(8,128)(2,1)}) %all-gather.25.cloned.1.call-update) | async-done | bytes 8388624 | tf_op jit(solution)/shard_map/all_gather | solution.py:95
  445.8 6.1 convolution_add_fusion.7
  451.9 143.4 %all-gather.27.cloned.1.call-done = bf16[4096,1024]{1,0:T(8,128)(2,1)} async-done(((bf16[1024,1024]{1,0:T(8,128)(2,1)}), bf16[4096,1024]{1,0:T(8,128)(2,1)}) %all-gather.27.cloned.1.call-update) | async-done | bytes 8388624 | tf_op jit(solution)/shard_map/all_gather | solution.py:97
  595.2 8.3 convert_reduce_fusion
  604.6 2.9 fusion.176
  609.7 4.3 convert_reduce_fusion.1
  614.0 3.6 multiply_reduce_fusion.3
  622.9 4.3 broadcast.392.clone2
  627.2 35.6 %while.83 = (s32[]{:T(128)}, f32[128,8,128]{0,2,1:T(8,128)S(1)}, f32[2,512,2048]{2,1,0:T(8,128)}, bf16[2,512,8,128]{3,1,2,0:T(8,128)(2,1)}, s32[128]{0:T(128)S(1...) while((s32[]{:T(128)}, f32[128,8,128]{0,2,1:T(8,128)S(1)}, ...), condition=%wide.region_32.33_spmd.clone, body=%wide.region_31.32_spmd.clone.sunk | while | flops 677183488 | bytes 60963544 | solution.py:252
  632.5 2.4 maximum_bitcast_fusion.5
  634.9 5.4 copy.272
  640.3 4.6 constant_dynamic-update-slice_fusion.5
  650.3 2.4 maximum_bitcast_fusion.5
  652.6 5.4 copy.272
  658.1 4.7 constant_dynamic-update-slice_fusion.5
  666.3 2.7 fusion.86
  673.3 4.7 broadcast.392.clone2.1
  678.0 36.3 %while.82 = (s32[]{:T(128)}, f32[128,8,128]{0,2,1:T(8,128)S(1)}, f32[2,512,2048]{2,1,0:T(8,128)}, bf16[2,512,8,128]{3,1,2,0:T(8,128)(2,1)}, s32[128]{0:T(128)S(1...) while((s32[]{:T(128)}, f32[128,8,128]{0,2,1:T(8,128)S(1)}, ...), condition=%wide.region_25.26_spmd.clone, body=%wide.region_24.25_spmd.clone.sunk | while | flops 677183488 | bytes 53623516 | solution.py:252
  683.4 2.4 maximum_bitcast_fusion.4
  685.8 5.8 copy.271
  691.6 4.9 constant_dynamic-update-slice_fusion.4
  701.8 2.4 maximum_bitcast_fusion.4
  704.2 5.5 copy.271
  709.7 4.6 constant_dynamic-update-slice_fusion.4
  716.1 2.8 convolution_add_fusion.9
  719.8 12.6 reduce-scatter.9.cloned.1.call-done
  733.7 73.7 %reduce-scatter.7.cloned.1.call-done = f32[128,2048]{1,0:T(8,128)} async-done(((f32[1024,2048]{1,0:T(8,128)}), f32[128,2048]{1,0:T(8,128)}) %reduce-scatter.7.cloned.1.call-update) | async-done | bytes 1048592 | tf_op jit(solution)/shard_map/reduce_scatter | solution.py:257
  811.6 6.4 convolution_add_fusion.6
  818.2 4.1 fusion.133
  822.4 9.1 convolution_add_fusion.4
  832.6 3.7 fusion.171
  836.3 8.2 convolution_add_fusion.5
  845.2 11.1 all-gather.7
  856.5 5.7 fusion.88
  862.3 5.2 fusion.89
  868.5 2.3 fusion.126
  870.8 2.5 fusion.120
  873.3 38.9 %all-reduce.9 = (f32[1024]{0:T(1024)S(1)}, f32[1024]{0:T(1024)S(1)}, f32[1024]{0:T(1024)S(1)}, f32[1024]{0:T(1024)S(1)}, f32[1024]{0:T(1024)S(1)}, /*index=5*/f3...) all-reduce(f32[1024]{0:T(1024)S(1)} %add.391, ...), channel_id=4, replica_groups=mesh['ctx'=8,'fsdp'=4] {'ctx','fsdp'}, use_global_device_ids=true, to_apply=%region_38.39.clone | all-reduce | flops 12288 | bytes 98304
  918.8 40.4 %reduce-scatter.13.cloned.1.call-done = f32[32,1024]{1,0:T(8,128)} async-done(((f32[1024,1024]{1,0:T(8,128)}), f32[32,1024]{1,0:T(8,128)}) %reduce-scatter.13.cloned.1.call-update) | async-done | bytes 131088 | tf_op jit(solution)/shard_map/reduce_scatter | solution.py:294
  959.2 160.6 %reduce-scatter.11.cloned.1.call-done = f32[32,3072]{1,0:T(8,128)} async-done(((f32[1024,3072]{1,0:T(8,128)}), f32[32,3072]{1,0:T(8,128)}) %reduce-scatter.11.cloned.1.call-update) | async-done | bytes 393232 | tf_op jit(solution)/shard_map/reduce_scatter | solution.py:291
  1119.8 366.4 %reduce-scatter.17.cloned.1.call-done = f32[128,1024]{1,0:T(8,128)} async-done(((f32[4096,1024]{1,0:T(8,128)}), f32[128,1024]{1,0:T(8,128)}) %reduce-scatter.17.cloned.1.call-update) | async-done | bytes 524304 | tf_op jit(solution)/shard_map/reduce_scatter | solution.py:300
  1486.1 365.0 %reduce-scatter.15.cloned.1.call-done = f32[32,4096]{1,0:T(8,128)} async-done(((f32[1024,4096]{1,0:T(8,128)}), f32[32,4096]{1,0:T(8,128)}) %reduce-scatter.15.cloned.1.call-update) | async-done | bytes 524304 | tf_op jit(solution)/shard_map/reduce_scatter | solution.py:298
  (439 shorter events, 105.5 us)
Async XLA Ops:
  7.2 23.8 %copy-start.9 = (bf16[2,128,1024]{2,1,0:T(8,128)(2,1)S(1)}, bf16[2,128,1024]{2,1,0:T(8,128)(2,1)}, u32[]{:S(2)}) copy-start(bf16[2,128,1024]{2,1,0:T(8,128)(2,1)} %param.28) | copy-start | bytes 1572868
  7.2 120.5 %all-gather.17.cloned.1.call-start = ((), (), s32[]{:S(2)}) async-start(), calls=%async_computation.6 | async-start | bytes 7864320 | tf_op jit(solution)/shard_map/all_gather | solution.py:88
  7.9 191.5 %all-gather.29.cloned.1.call-start = ((), (), s32[]{:S(2)}) async-start(), calls=%async_computation.12 | async-start | bytes 2359296 | tf_op jit(solution)/shard_map/all_gather | solution.py:134
  21.9 127.7 %copy-start.50 = (f32[4,1,256]{2,1,0:T(1,128)}, f32[4,1,256]{2,1,0:T(1,128)S(1)}, u32[]{:S(2)}) copy-start(f32[4,1,256]{2,1,0:T(1,128)S(1)} %convert_element_type.245) | copy-start | bytes 12292
  29.7 119.9 %copy-start.48 = (f32[4,1,256]{2,1,0:T(1,128)}, f32[4,1,256]{2,1,0:T(1,128)S(1)}, u32[]{:S(2)}) copy-start(f32[4,1,256]{2,1,0:T(1,128)S(1)} %convert_element_type.244) | copy-start | bytes 12292
  30.9 100.6 %copy-start.57 = (f32[128]{0:T(128)}, f32[128]{0:T(128)S(1)}, u32[]{:S(2)}) copy-start(f32[128]{0:T(128)S(1)} %get-tuple-element.905) | copy-start | bytes 1540
  30.9 118.7 %copy-start.63 = (f32[128]{0:T(128)}, f32[128]{0:T(128)S(1)}, u32[]{:S(2)}) copy-start(f32[128]{0:T(128)S(1)} %get-tuple-element.906) | copy-start | bytes 1540
  31.2 100.3 %copy-start.79 = (f32[128]{0:T(128)}, f32[128]{0:T(128)S(1)}, u32[]{:S(2)}) copy-start(f32[128]{0:T(128)S(1)} %add_rsqrt_fusion.1) | copy-start | bytes 1540
  127.7 4.7 copy-start.86
  127.7 4.8 copy-start.87
  132.3 71.0 %all-gather.31.cloned.1.call-start = ((), (), s32[]{:S(2)}) async-start(), calls=%async_computation.13 | async-start | bytes 2359296 | tf_op jit(solution)/shard_map/all_gather | solution.py:135
  155.0 63.8 %all-gather.21.cloned.1.call-start = ((), (), s32[]{:S(2)}) async-start(), calls=%async_computation.8 | async-start | bytes 2359296 | tf_op jit(solution)/shard_map/all_gather | solution.py:135
  155.5 92.9 %all-gather.19.cloned.1.call-start = ((), (), s32[]{:S(2)}) async-start(), calls=%async_computation.7 | async-start | bytes 2359296 | tf_op jit(solution)/shard_map/all_gather | solution.py:134
  157.4 138.4 %all-gather.23.cloned.1.call-start = ((), (), s32[]{:S(2)}) async-start(), calls=%async_computation.9 | async-start | bytes 2621440 | tf_op jit(solution)/shard_map/all_gather | solution.py:91
  158.0 27.2 %copy-start.84 = (bf16[1024]{0:T(1024)(128)(2,1)S(1)}, bf16[1024]{0:T(1024)(128)(2,1)}, u32[]{:S(2)}) copy-start(bf16[1024]{0:T(1024)(128)(2,1)} %param.40) | copy-start | bytes 6148
  158.0 287.7 %all-gather.25.cloned.1.call-start = ((), (), s32[]{:S(2)}) async-start(), calls=%async_computation.10 | async-start | bytes 10485760 | tf_op jit(solution)/shard_map/all_gather | solution.py:95
  158.8 436.4 %all-gather.27.cloned.1.call-start = ((), (), s32[]{:S(2)}) async-start(), calls=%async_computation.11 | async-start | bytes 10485760 | tf_op jit(solution)/shard_map/all_gather | solution.py:97
  159.5 572.9 %reduce-scatter.9.cloned.1.call-start = ((), (), s32[]{:S(2)}) async-start(), calls=%async_computation.15 | async-start | bytes 9437184 | tf_op jit(solution)/shard_map/reduce_scatter | solution.py:257
  168.1 439.4 %copy-start.52 = (f32[4,1,256]{2,1,0:T(1,128)}, f32[4,1,256]{2,1,0:T(1,128)S(1)}, u32[]{:S(2)}) copy-start(f32[4,1,256]{2,1,0:T(1,128)S(1)} %convert_element_type.250) | copy-start | bytes 12292
  176.9 440.7 %copy-start.46 = (f32[4,1,256]{2,1,0:T(1,128)}, f32[4,1,256]{2,1,0:T(1,128)S(1)}, u32[]{:S(2)}) copy-start(f32[4,1,256]{2,1,0:T(1,128)S(1)} %convert_element_type.249) | copy-start | bytes 12292
  281.8 17.2 copy-start.42
  298.2 319.4 %copy-start.59 = (f32[128]{0:T(128)}, f32[128]{0:T(128)S(1)}, u32[]{:S(2)}) copy-start(f32[128]{0:T(128)S(1)} %broadcast_multiply_fusion.12) | copy-start | bytes 1540
  299.5 318.1 %copy-start.7 = (f32[128,1024]{1,0:T(8,128)}, f32[128,1024]{1,0:T(8,128)S(1)}, u32[]{:S(2)}) copy-start(f32[128,1024]{1,0:T(8,128)S(1)} %get-tuple-element.894) | copy-start | bytes 1572868
  299.6 318.1 %copy-start.61 = (f32[128]{0:T(128)}, f32[128]{0:T(128)S(1)}, u32[]{:S(2)}) copy-start(f32[128]{0:T(128)S(1)} %broadcast_multiply_fusion.10) | copy-start | bytes 1540
  299.8 317.9 %copy-start.67 = (f32[128]{0:T(128)}, f32[128]{0:T(128)S(1)}, u32[]{:S(2)}) copy-start(f32[128]{0:T(128)S(1)} %add_rsqrt_fusion.2) | copy-start | bytes 1540
  299.8 317.9 %copy-start.65 = (f32[128]{0:T(128)}, f32[128]{0:T(128)S(1)}, u32[]{:S(2)}) copy-start(f32[128]{0:T(128)S(1)} %add_rsqrt_fusion) | copy-start | bytes 1540
  445.8 149.5 %copy-start.45 = (bf16[2,128,1024]{2,1,0:T(8,128)(2,1)S(1)}, bf16[2,128,1024]{2,1,0:T(8,128)(2,1)}, u32[]{:S(2)}) copy-start(bf16[2,128,1024]{2,1,0:T(8,128)(2,1)} %param.43) | copy-start | bytes 1572868
  595.2 9.3 copy-start
  622.9 4.3 copy-start.14
  662.8 144.7 %reduce-scatter.7.cloned.1.call-start = ((), (), s32[]{:S(2)}) async-start(), calls=%async_computation.14 | async-start | bytes 9437184 | tf_op jit(solution)/shard_map/reduce_scatter | solution.py:257
  714.4 244.8 %reduce-scatter.13.cloned.1.call-start = ((), (), s32[]{:S(2)}) async-start(), calls=%async_computation.17 | async-start | bytes 4325376 | tf_op jit(solution)/shard_map/reduce_scatter | solution.py:294
  719.0 400.8 %reduce-scatter.11.cloned.1.call-start = ((), (), s32[]{:S(2)}) async-start(), calls=%async_computation.16 | async-start | bytes 12976128 | tf_op jit(solution)/shard_map/reduce_scatter | solution.py:291
  719.4 92.1 %copy-start.40 = (bf16[128,1024]{1,0:T(8,128)(2,1)}, bf16[128,1024]{1,0:T(8,128)(2,1)S(1)}, u32[]{:S(2)}) copy-start(bf16[128,1024]{1,0:T(8,128)(2,1)S(1)} %copy.214) | copy-start | bytes 786436
  719.4 90.2 %copy-start.10 = (bf16[2,128,1024]{2,1,0:T(8,128)(2,1)S(1)}, bf16[2,128,1024]{2,1,0:T(8,128)(2,1)}, u32[]{:S(2)}) copy-start(bf16[2,128,1024]{2,1,0:T(8,128)(2,1)} %param.28) | copy-start | bytes 1572868
  719.4 90.1 %copy-start.49 = (f32[4,1,256]{2,1,0:T(1,128)S(1)}, f32[4,1,256]{2,1,0:T(1,128)}, u32[]{:S(2)}) copy-start(f32[4,1,256]{2,1,0:T(1,128)} %copy-done.48) | copy-start | bytes 12292
  719.4 90.1 %copy-start.51 = (f32[4,1,256]{2,1,0:T(1,128)S(1)}, f32[4,1,256]{2,1,0:T(1,128)}, u32[]{:S(2)}) copy-start(f32[4,1,256]{2,1,0:T(1,128)} %copy-done.50) | copy-start | bytes 12292
  719.4 90.1 %copy-start.64 = (f32[128]{0:T(128)S(1)}, f32[128]{0:T(128)}, u32[]{:S(2)}) copy-start(f32[128]{0:T(128)} %copy-done.63) | copy-start | bytes 1540
  719.4 90.1 %copy-start.82 = (f32[128]{0:T(128)S(1)}, f32[128]{0:T(128)}, u32[]{:S(2)}) copy-start(f32[128]{0:T(128)} %copy-done.81) | copy-start | bytes 1540
  719.8 91.7 %copy-start.55 = (bf16[128,1024]{1,0:T(8,128)(2,1)}, bf16[128,1024]{1,0:T(8,128)(2,1)S(1)}, u32[]{:S(2)}) copy-start(bf16[128,1024]{1,0:T(8,128)(2,1)S(1)} %copy.213) | copy-start | bytes 786436
  733.7 77.8 %copy-start.32 = (bf16[128,2048]{1,0:T(8,128)(2,1)}, bf16[128,2048]{1,0:T(8,128)(2,1)S(1)}, u32[]{:S(2)}) copy-start(bf16[128,2048]{1,0:T(8,128)(2,1)S(1)} %convert.17) | copy-start | bytes 1572868
  818.0 668.2 %reduce-scatter.17.cloned.1.call-start = ((), (), s32[]{:S(2)}) async-start(), calls=%async_computation.19 | async-start | bytes 17301504 | tf_op jit(solution)/shard_map/reduce_scatter | solution.py:300
  831.6 4.7 copy-start.8
  831.6 4.7 copy-start.36
  831.6 4.7 copy-start.62
  831.6 4.7 copy-start.66
  831.6 1019.5 %reduce-scatter.15.cloned.1.call-start = ((), (), s32[]{:S(2)}) async-start(), calls=%async_computation.18 | async-start | bytes 17301504 | tf_op jit(solution)/shard_map/reduce_scatter | solution.py:298
  844.5 11.8 copy-start.77
  844.5 11.8 copy-start.78
  844.5 11.8 copy-start.71
  844.5 11.8 copy-start.72
  844.5 11.9 copy-start.69
  844.6 11.9 copy-start.70
  844.6 11.9 copy-start.75
  844.6 11.9 copy-start.76
  844.6 11.9 copy-start.73
  844.6 11.9 copy-start.74
  856.5 5.8 copy-start.24
  856.5 12.0 slice-start
  862.3 6.0 copy-start.33
  862.3 6.1 copy-start.39
  862.3 6.2 slice-start.1
  862.3 6.2 copy-start.41
  870.8 46.7 %copy-start.29 = (f32[128,1024]{1,0:T(8,128)S(1)}, f32[128,1024]{1,0:T(8,128)}, u32[]{:S(2)}) copy-start(f32[128,1024]{1,0:T(8,128)} %copy-done.27) | copy-start | bytes 1572868
  870.8 46.7 %copy-start.31 = (f32[128,1024]{1,0:T(8,128)S(1)}, f32[128,1024]{1,0:T(8,128)}, u32[]{:S(2)}) copy-start(f32[128,1024]{1,0:T(8,128)} %get-tuple-element.879) | copy-start | bytes 1572868
  (57 other events, 104.6 us)
Sparse Core Ops, SparseCore 0:
  9.6 118.0 all-gather.16
  132.5 26.1 all-gather.28
  161.2 27.8 all-gather.30
  190.8 27.8 all-gather.20
  220.5 27.8 all-gather.18
  249.8 45.9 all-gather.22
  297.4 148.3 all-gather.24
  447.3 147.8 all-gather.26
  662.9 69.4 reduce-scatter.8
  736.1 71.2 reduce-scatter.6
  810.3 148.8 reduce-scatter.12
  965.6 154.0 reduce-scatter.10
  1122.7 363.3 reduce-scatter.16
  1488.9 362.1 reduce-scatter.14
where the time goes:
time: 1860 us
  waiting for transfers between devices  1460 us (78%)
  matrix products  130 us (7%)
  blocking collectives  125 us (7%)
  local copies, waits for them, and re-layouts  97.7 us (5%)
  other arithmetic  28.4 us (2%)
    reduce_scatter x1, waiting for transfers between devices, per_device(): lax.psum_scatter(totals[11], ('ctx', 'fsdp'), scatter_dimension=0, tiled=...  366 us
    reduce_scatter x1, waiting for transfers between devices, per_device(): lax.psum_scatter(totals[9], ('ctx', 'fsdp'), scatter_dimension=0, tiled=T...  365 us
    reduce_scatter x1, waiting for transfers between devices, per_device(): lax.psum_scatter(totals[2], ('ctx', 'fsdp'), scatter_dimension=0, tiled=T...  161 us
    all_gather x1, waiting for transfers between devices, per_device(): lax.all_gather(w_up, 'fsdp', axis=0, tiled=True)  146 us
    all_gather x1, waiting for transfers between devices, per_device(): lax.all_gather(w_down, 'fsdp', axis=0, tiled=True)  143 us
    all_gather x1, waiting for transfers between devices, per_device(): lax.all_gather(w_qkv, 'fsdp', axis=0, tiled=True)  96.4 us
    reduce_scatter x2, waiting for transfers between devices, per_device(): lax.psum_scatter(key_terms.reshape(seq_len, 2 * D), 'ctx', scatter_dimens...  86.3 us
    dynamic_update_slice x8, local copies, waits for them, and re-layouts, per_device(): lax.scan(backward_step, jnp.zeros((tokens, HEADS, HEAD_DIM), jnp.float32)...  41 us
  transfers between devices with their start and end apart: 14, of which 12 were waited for; matrix products, arithmetic and copies ran while one was open for 9% of the time, Pallas kernels for 0%

commit v1 on v0

--- a/solution.py
+++ b/solution.py
@@ -1,3 +1,4 @@
+import functools
 import math
 import jax
 import jax.numpy as jnp
@@ -11,6 +12,35 @@
 NEG_LARGE = -1e30
 GELU_C = math.sqrt(2.0 / math.pi)
 GELU_K = 0.044715
+
+
+def tails_form(s0, which_dim):
+    s0 = jnp.moveaxis(s0, 0, which_dim)
+    out_arr = s0.shape
+    e_next = s0.reshape(
+        *out_arr[:which_dim], out_arr[which_dim] * out_arr[which_dim + 1], *out_arr[which_dim + 2 :]
+    )
+    return e_next
+
+
+def trace_ways_now(original, which_axis):
+    devs = lax.axis_size(which_axis)
+    moved = original[None]
+    for t in range(devs.bit_length() - 1):
+        tmp = 1 << t
+        known = lax.ppermute(moved, axis_name=which_axis, perm=[(s, s ^ tmp) for s in range(devs)])
+        p_next = jnp.stack([moved, known], 0)
+        fresh = lax.axis_index(which_axis) >> t & 1
+        moved = jnp.where(fresh == 0, p_next, p_next[::-1]).reshape(-1, *original.shape)
+    return moved
+
+
+def trace_quotas(here_x, block_here, axis_no):
+    r1 = tails_form(trace_ways_now(here_x, block_here), axis_no)
+    return r1
+
+
+_draw_strips_all = functools.partial(trace_quotas, block_here="fsdp", axis_no=0)
 
 
 def gelu_tanh(values):
@@ -92,7 +122,7 @@
         lax.all_gather(b_out, "fsdp", axis=0, tiled=True),
         lax.all_gather(ln2_gain, "fsdp", axis=0, tiled=True),
         lax.all_gather(ln2_shift, "fsdp", axis=0, tiled=True),
-        lax.all_gather(w_up, "fsdp", axis=0, tiled=True),
+        _draw_strips_all(w_up),
         lax.all_gather(b_up, "fsdp", axis=0, tiled=True),
         lax.all_gather(w_down, "fsdp", axis=0, tiled=True),
         lax.all_gather(b_down, "fsdp", axis=0, tiled=True),

time: 1860 us -> 1930 us (1.038)
  blocking collectives: 125 us -> 458 us
  waiting for transfers between devices: 1460 us -> 1160 us
  other arithmetic: 28.4 us -> 56.3 us
    all_gather x1, blocking collectives: 8.86 us -> 241 us  [per_device(): lax.all_gather(ln2_gain, 'fsdp', axis=0, tiled=True)]
    all_gather x1 -> x0, waiting for transfers between devices: 146 us -> none  [per_device(): lax.all_gather(w_up, 'fsdp', axis=0, tiled=True)]
    all_gather x1, waiting for transfers between devices: 143 us -> 0.01 us  [per_device(): lax.all_gather(w_down, 'fsdp', axis=0, tiled=True)]
    all_gather x1, blocking collectives: 8.29 us -> 110 us  [per_device(): lax.all_gather(ln2_shift, 'fsdp', axis=0, tiled=True)]
    ppermute x0 -> x2, waiting for transfers between devices: none -> 43.3 us  [trace_ways_now(): lax.ppermute(moved, axis_name=which_axis, perm=[(s, s ^ tmp) for s in ran...]
    all_gather x2, waiting for transfers between devices: 27.1 us -> 0.04 us  [per_device(): lax.all_gather(key_low, 'ctx', axis=0, tiled=True)]
  transfers between devices with their start and end apart: 14 -> 15, of which waited for: 12 -> 8; matrix products, arithmetic and copies ran while one was open for 9% -> 10% of each run, Pallas kernels for 0% -> 0%
where the time goes in v1:
time: 1930 us
  waiting for transfers between devices  1160 us (60%)
  blocking collectives  458 us (24%)
  matrix products  136 us (7%)
  local copies, waits for them, and re-layouts  96.3 us (5%)
  other arithmetic  56.3 us (3%)
    reduce_scatter x1, waiting for transfers between devices, per_device(): lax.psum_scatter(totals[11], ('ctx', 'fsdp'), scatter_dimension=0, tiled=...  366 us
    reduce_scatter x1, waiting for transfers between devices, per_device(): lax.psum_scatter(totals[9], ('ctx', 'fsdp'), scatter_dimension=0, tiled=T...  365 us
    all_gather x1, blocking collectives, per_device(): lax.all_gather(ln2_gain, 'fsdp', axis=0, tiled=True)  241 us
    reduce_scatter x1, waiting for transfers between devices, per_device(): lax.psum_scatter(totals[2], ('ctx', 'fsdp'), scatter_dimension=0, tiled=T...  161 us
    all_gather x1, blocking collectives, per_device(): lax.all_gather(ln2_shift, 'fsdp', axis=0, tiled=True)  110 us
    all_gather x1, waiting for transfers between devices, per_device(): lax.all_gather(w_qkv, 'fsdp', axis=0, tiled=True)  96.4 us
    reduce_scatter x2, waiting for transfers between devices, per_device(): lax.psum_scatter(key_terms.reshape(seq_len, 2 * D), 'ctx', scatter_dimens...  86.2 us
    ppermute x2, waiting for transfers between devices, trace_ways_now(): lax.ppermute(moved, axis_name=which_axis, perm=[(s, s ^ tmp) for s in ran...  43.3 us
  transfers between devices with their start and end apart: 15, of which 8 were waited for; matrix products, arithmetic and copies ran while one was open for 10% of the time, Pallas kernels for 0%

profile of v1, /device:TPU:0, one launch (start us, length us, event | category | flops | bytes accessed | tf_op | source)
XLA Modules:
  0.0 1926.0 jit_solution(17465133771471344634)
XLA Ops:
  9.3 12.6 all-gather.1
  21.9 7.8 all-gather
  31.3 96.4 %all-gather.16.cloned.1.call-done = bf16[1024,3072]{1,0:T(8,128)(2,1)} async-done(((bf16[256,3072]{1,0:T(8,128)(2,1)}), bf16[1024,3072]{1,0:T(8,128)(2,1)}) %all-gather.16.cloned.1.call-update) | async-done | bytes 6291472 | tf_op jit(solution)/shard_map/all_gather | solution.py:118
  127.7 3.9 fusion.171
  132.4 7.9 all-gather.3
  140.4 9.2 all-gather.2
  149.7 3.9 fusion.168
  158.5 43.3 %collective-permute-done = bf16[1,256,4096]{2,1,0:T(8,128)(2,1)S(1)} collective-permute-done((bf16[1,256,4096]{2,1,0:T(8,128)(2,1)}, bf16[1,256,4096]{2,1,0:T(8,128)(2,1)S(1)}, u32[]{:S(2)}, u32[]{:S(2)}) %collective-permute-start) | collective-permute-done | bytes 2097184 | tf_op jit(solution)/shard_map/ppermute | solution.py:31
  203.8 4.7 fusion.71
  209.2 110.4 %all-gather.6 = bf16[4,1,256]{2,1,0:T(2,128)(2,1)S(1)} all-gather(bf16[1,1,256]{2,1,0:T(2,128)(2,1)S(1)} %reshape.399), channel_id=1, replica_groups=mesh['ctx'=8,'fsdp'=4] {'fsdp'}, dimensions={0}, use_global_device_ids=true | all-gather | bytes 2560 | tf_op jit(solution)/shard_map/all_gather | solution.py:124
  319.6 240.7 %all-gather.5 = bf16[4,1,256]{2,1,0:T(2,128)(2,1)S(1)} all-gather(bf16[1,1,256]{2,1,0:T(2,128)(2,1)S(1)} %reshape.397), channel_id=1, replica_groups=mesh['ctx'=8,'fsdp'=4] {'fsdp'}, dimensions={0}, use_global_device_ids=true | all-gather | bytes 2560 | tf_op jit(solution)/shard_map/all_gather | solution.py:123
  560.4 7.6 all-gather.4
  568.0 12.2 all_gather.59
  580.5 7.5 pad_maximum_fusion
  587.9 13.6 reverse_select_fusion
  603.3 2.2 copy.257
  611.2 2.2 copy.256
  613.8 2.2 copy.255
  617.8 5.5 while.80
  623.3 10.0 while.81
  635.1 4.9 while.78
  640.0 7.5 while.79
  648.4 2.4 fusion.175
  652.4 6.1 convolution_add_fusion.7
  658.5 8.1 convert_reduce_fusion
  667.7 6.4 fusion.178
  674.1 4.9 convolution_add_fusion.8
  679.1 4.3 convert_reduce_fusion.1
  683.4 3.7 multiply_reduce_fusion.3
  692.4 4.3 broadcast.395.clone2
  696.7 35.4 %while.83 = (s32[]{:T(128)}, f32[128,8,128]{0,2,1:T(8,128)S(1)}, f32[2,512,2048]{2,1,0:T(8,128)}, bf16[2,512,8,128]{3,1,2,0:T(8,128)(2,1)}, s32[128]{0:T(128)S(1...) while((s32[]{:T(128)}, f32[128,8,128]{0,2,1:T(8,128)S(1)}, ...), condition=%wide.region_32.33_spmd.clone, body=%wide.region_31.32_spmd.clone.sunk | while | flops 677183488 | bytes 60963544 | solution.py:282
  702.0 2.4 maximum_bitcast_fusion.5
  704.4 5.4 copy.272
  709.7 4.6 constant_dynamic-update-slice_fusion.5
  719.7 2.4 maximum_bitcast_fusion.5
  722.0 5.4 copy.272
  727.4 4.7 constant_dynamic-update-slice_fusion.5
  735.6 2.6 fusion.88
  742.5 4.5 broadcast.395.clone2.1
  747.0 36.1 %while.82 = (s32[]{:T(128)}, f32[128,8,128]{0,2,1:T(8,128)S(1)}, f32[2,512,2048]{2,1,0:T(8,128)}, bf16[2,512,8,128]{3,1,2,0:T(8,128)(2,1)}, s32[128]{0:T(128)S(1...) while((s32[]{:T(128)}, f32[128,8,128]{0,2,1:T(8,128)S(1)}, ...), condition=%wide.region_25.26_spmd.clone, body=%wide.region_24.25_spmd.clone.sunk | while | flops 677183488 | bytes 53623516 | solution.py:282
  752.7 2.5 maximum_bitcast_fusion.4
  755.1 5.4 copy.271
  760.6 4.9 constant_dynamic-update-slice_fusion.4
  770.7 2.5 maximum_bitcast_fusion.4
  773.2 5.4 copy.271
  778.5 4.6 constant_dynamic-update-slice_fusion.4
  785.0 2.8 convolution_add_fusion.9
  788.6 12.4 reduce-scatter.9.cloned.1.call-done
  802.3 73.9 %reduce-scatter.7.cloned.1.call-done = f32[128,2048]{1,0:T(8,128)} async-done(((f32[1024,2048]{1,0:T(8,128)}), f32[128,2048]{1,0:T(8,128)}) %reduce-scatter.7.cloned.1.call-update) | async-done | bytes 1048592 | tf_op jit(solution)/shard_map/reduce_scatter | solution.py:287
  880.3 6.4 convolution_add_fusion.6
  886.9 4.1 fusion.135
  891.1 9.1 convolution_add_fusion.4
  901.2 3.7 fusion.173
  905.0 8.2 convolution_add_fusion.5
  913.9 11.1 all-gather.7
  925.1 5.7 fusion.90
  930.9 5.2 fusion.91
  937.1 2.3 fusion.128
  939.4 2.5 fusion.122
  941.9 38.1 %all-reduce.9 = (f32[1024]{0:T(1024)S(1)}, f32[1024]{0:T(1024)S(1)}, f32[1024]{0:T(1024)S(1)}, f32[1024]{0:T(1024)S(1)}, f32[1024]{0:T(1024)S(1)}, /*index=5*/f3...) all-reduce(f32[1024]{0:T(1024)S(1)} %add.391, ...), channel_id=4, replica_groups=mesh['ctx'=8,'fsdp'=4] {'ctx','fsdp'}, use_global_device_ids=true, to_apply=%region_38.39.clone | all-reduce | flops 12288 | bytes 98304
  986.6 40.4 %reduce-scatter.13.cloned.1.call-done = f32[32,1024]{1,0:T(8,128)} async-done(((f32[1024,1024]{1,0:T(8,128)}), f32[32,1024]{1,0:T(8,128)}) %reduce-scatter.13.cloned.1.call-update) | async-done | bytes 131088 | tf_op jit(solution)/shard_map/reduce_scatter | solution.py:324
  1027.0 160.9 %reduce-scatter.11.cloned.1.call-done = f32[32,3072]{1,0:T(8,128)} async-done(((f32[1024,3072]{1,0:T(8,128)}), f32[32,3072]{1,0:T(8,128)}) %reduce-scatter.11.cloned.1.call-update) | async-done | bytes 393232 | tf_op jit(solution)/shard_map/reduce_scatter | solution.py:321
  1187.9 366.2 %reduce-scatter.17.cloned.1.call-done = f32[128,1024]{1,0:T(8,128)} async-done(((f32[4096,1024]{1,0:T(8,128)}), f32[128,1024]{1,0:T(8,128)}) %reduce-scatter.17.cloned.1.call-update) | async-done | bytes 524304 | tf_op jit(solution)/shard_map/reduce_scatter | solution.py:330
  1554.1 365.2 %reduce-scatter.15.cloned.1.call-done = f32[32,4096]{1,0:T(8,128)} async-done(((f32[1024,4096]{1,0:T(8,128)}), f32[32,4096]{1,0:T(8,128)}) %reduce-scatter.15.cloned.1.call-update) | async-done | bytes 524304 | tf_op jit(solution)/shard_map/reduce_scatter | solution.py:328
  (451 shorter events, 104.8 us)
Async XLA Ops:
  7.2 23.8 %copy-start.8 = (bf16[2,128,1024]{2,1,0:T(8,128)(2,1)S(1)}, bf16[2,128,1024]{2,1,0:T(8,128)(2,1)}, u32[]{:S(2)}) copy-start(bf16[2,128,1024]{2,1,0:T(8,128)(2,1)} %param.28) | copy-start | bytes 1572868
  7.2 120.5 %all-gather.16.cloned.1.call-start = ((), (), s32[]{:S(2)}) async-start(), calls=%async_computation.6 | async-start | bytes 7864320 | tf_op jit(solution)/shard_map/all_gather | solution.py:118
  7.9 595.4 %all-gather.26.cloned.1.call-start = ((), (), s32[]{:S(2)}) async-start(), calls=%async_computation.11 | async-start | bytes 2359296 | tf_op jit(solution)/shard_map/all_gather | solution.py:164
  21.9 127.7 %copy-start.49 = (f32[4,1,256]{2,1,0:T(1,128)}, f32[4,1,256]{2,1,0:T(1,128)S(1)}, u32[]{:S(2)}) copy-start(f32[4,1,256]{2,1,0:T(1,128)S(1)} %convert_element_type.245) | copy-start | bytes 12292
  29.7 119.9 %copy-start.47 = (f32[4,1,256]{2,1,0:T(1,128)}, f32[4,1,256]{2,1,0:T(1,128)S(1)}, u32[]{:S(2)}) copy-start(f32[4,1,256]{2,1,0:T(1,128)S(1)} %convert_element_type.244) | copy-start | bytes 12292
  30.9 100.7 %copy-start.58 = (f32[128]{0:T(128)}, f32[128]{0:T(128)S(1)}, u32[]{:S(2)}) copy-start(f32[128]{0:T(128)S(1)} %get-tuple-element.907) | copy-start | bytes 1540
  30.9 118.7 %copy-start.64 = (f32[128]{0:T(128)}, f32[128]{0:T(128)S(1)}, u32[]{:S(2)}) copy-start(f32[128]{0:T(128)S(1)} %get-tuple-element.908) | copy-start | bytes 1540
  31.2 100.3 %copy-start.80 = (f32[128]{0:T(128)}, f32[128]{0:T(128)S(1)}, u32[]{:S(2)}) copy-start(f32[128]{0:T(128)S(1)} %add_rsqrt_fusion.1) | copy-start | bytes 1540
  127.7 4.8 copy-start.88
  132.4 474.9 %all-gather.28.cloned.1.call-start = ((), (), s32[]{:S(2)}) async-start(), calls=%async_computation.12 | async-start | bytes 2359296 | tf_op jit(solution)/shard_map/all_gather | solution.py:165
  155.2 456.0 %all-gather.20.cloned.1.call-start = ((), (), s32[]{:S(2)}) async-start(), calls=%async_computation.8 | async-start | bytes 2359296 | tf_op jit(solution)/shard_map/all_gather | solution.py:165
  155.8 458.0 %all-gather.18.cloned.1.call-start = ((), (), s32[]{:S(2)}) async-start(), calls=%async_computation.7 | async-start | bytes 2359296 | tf_op jit(solution)/shard_map/all_gather | solution.py:164
  157.6 490.8 %all-gather.22.cloned.1.call-start = ((), (), s32[]{:S(2)}) async-start(), calls=%async_computation.9 | async-start | bytes 2621440 | tf_op jit(solution)/shard_map/all_gather | solution.py:121
  157.7 44.1 %collective-permute-start = (bf16[1,256,4096]{2,1,0:T(8,128)(2,1)}, bf16[1,256,4096]{2,1,0:T(8,128)(2,1)S(1)}, u32[]{:S(2)}, u32[]{:S(2)}) collective-permute-start(bf16[1,256,4096]{2,1,0:T(8,128)(2,1)} %bitcast.491), channel_id=1, source_target_pairs={{0,1},{1,0},{2,3},{3,2},{4,5},{5,4},{6,7},{7,6},{8,9},{9,8},{10,11... | collective-permute-start | bytes 6291464 | tf_op jit(solution)/shard_map/ppermute | solution.py:31
  158.5 500.0 %all-gather.24.cloned.1.call-start = ((), (), s32[]{:S(2)}) async-start(), calls=%async_computation.10 | async-start | bytes 10485760 | tf_op jit(solution)/shard_map/all_gather | solution.py:127
  208.4 359.5 %copy-start.85 = (bf16[1024]{0:T(1024)(128)(2,1)S(1)}, bf16[1024]{0:T(1024)(128)(2,1)}, u32[]{:S(2)}) copy-start(bf16[1024]{0:T(1024)(128)(2,1)} %param.40) | copy-start | bytes 6148
  208.4 371.7 %copy-start.86 = (s32[2,16]{1,0:T(2,128)S(1)}, s32[2,16]{1,0:T(2,128)}, u32[]{:S(2)}) copy-start(s32[2,16]{1,0:T(2,128)} %param.29) | copy-start | bytes 388
  208.5 372.0 %collective-permute-start.1 = (bf16[2,256,4096]{2,1,0:T(8,128)(2,1)}, bf16[2,256,4096]{2,1,0:T(8,128)(2,1)}, u32[]{:S(2)}, u32[]{:S(2)}) collective-permute-start(bf16[2,256,4096]{2,1,0:T(8,128)(2,1)} %get-tuple-element.867), channel_id=1, source_target_pairs={{0,2},{1,3},{2,0},{3,1},{4,6},{5,7},{6,4},{7,5},{8,10},{9,11},{10,... | collective-permute-start | bytes 12582920 | tf_op jit(solution)/shard_map/ppermute | solution.py:31
  209.0 592.0 %reduce-scatter.9.cloned.1.call-start = ((), (), s32[]{:S(2)}) async-start(), calls=%async_computation.14 | async-start | bytes 9437184 | tf_op jit(solution)/shard_map/reduce_scatter | solution.py:287
  319.6 354.5 %copy-start.51 = (f32[4,1,256]{2,1,0:T(1,128)}, f32[4,1,256]{2,1,0:T(1,128)S(1)}, u32[]{:S(2)}) copy-start(f32[4,1,256]{2,1,0:T(1,128)S(1)} %convert_element_type.250) | copy-start | bytes 12292
  560.4 126.7 %copy-start.45 = (f32[4,1,256]{2,1,0:T(1,128)}, f32[4,1,256]{2,1,0:T(1,128)S(1)}, u32[]{:S(2)}) copy-start(f32[4,1,256]{2,1,0:T(1,128)S(1)} %convert_element_type.249) | copy-start | bytes 12292
  587.9 13.6 copy-start.55
  587.9 15.3 copy-start.54
  650.8 36.3 %copy-start.60 = (f32[128]{0:T(128)}, f32[128]{0:T(128)S(1)}, u32[]{:S(2)}) copy-start(f32[128]{0:T(128)S(1)} %broadcast_multiply_fusion.12) | copy-start | bytes 1540
  652.1 35.0 %copy-start.6 = (f32[128,1024]{1,0:T(8,128)}, f32[128,1024]{1,0:T(8,128)S(1)}, u32[]{:S(2)}) copy-start(f32[128,1024]{1,0:T(8,128)S(1)} %get-tuple-element.896) | copy-start | bytes 1572868
  652.1 35.0 %copy-start.62 = (f32[128]{0:T(128)}, f32[128]{0:T(128)S(1)}, u32[]{:S(2)}) copy-start(f32[128]{0:T(128)S(1)} %broadcast_multiply_fusion.10) | copy-start | bytes 1540
  652.4 34.8 %copy-start.68 = (f32[128]{0:T(128)}, f32[128]{0:T(128)S(1)}, u32[]{:S(2)}) copy-start(f32[128]{0:T(128)S(1)} %add_rsqrt_fusion.2) | copy-start | bytes 1540
  652.4 34.8 %copy-start.66 = (f32[128]{0:T(128)}, f32[128]{0:T(128)S(1)}, u32[]{:S(2)}) copy-start(f32[128]{0:T(128)S(1)} %add_rsqrt_fusion) | copy-start | bytes 1540
  652.4 6.1 copy-start.44
  667.7 6.4 copy-start.11
  667.7 11.3 slice-start.4
  674.1 4.9 slice-start.5
  674.1 9.3 slice-start
  732.1 144.0 %reduce-scatter.7.cloned.1.call-start = ((), (), s32[]{:S(2)}) async-start(), calls=%async_computation.13 | async-start | bytes 9437184 | tf_op jit(solution)/shard_map/reduce_scatter | solution.py:287
  783.2 243.8 %reduce-scatter.13.cloned.1.call-start = ((), (), s32[]{:S(2)}) async-start(), calls=%async_computation.16 | async-start | bytes 4325376 | tf_op jit(solution)/shard_map/reduce_scatter | solution.py:324
  787.8 400.1 %reduce-scatter.11.cloned.1.call-start = ((), (), s32[]{:S(2)}) async-start(), calls=%async_computation.15 | async-start | bytes 12976128 | tf_op jit(solution)/shard_map/reduce_scatter | solution.py:321
  788.2 92.0 %copy-start.39 = (bf16[128,1024]{1,0:T(8,128)(2,1)}, bf16[128,1024]{1,0:T(8,128)(2,1)S(1)}, u32[]{:S(2)}) copy-start(bf16[128,1024]{1,0:T(8,128)(2,1)S(1)} %copy.214) | copy-start | bytes 786436
  788.2 90.0 %copy-start.9 = (bf16[2,128,1024]{2,1,0:T(8,128)(2,1)S(1)}, bf16[2,128,1024]{2,1,0:T(8,128)(2,1)}, u32[]{:S(2)}) copy-start(bf16[2,128,1024]{2,1,0:T(8,128)(2,1)} %param.28) | copy-start | bytes 1572868
  788.2 90.0 %copy-start.48 = (f32[4,1,256]{2,1,0:T(1,128)S(1)}, f32[4,1,256]{2,1,0:T(1,128)}, u32[]{:S(2)}) copy-start(f32[4,1,256]{2,1,0:T(1,128)} %copy-done.47) | copy-start | bytes 12292
  788.2 90.0 %copy-start.50 = (f32[4,1,256]{2,1,0:T(1,128)S(1)}, f32[4,1,256]{2,1,0:T(1,128)}, u32[]{:S(2)}) copy-start(f32[4,1,256]{2,1,0:T(1,128)} %copy-done.49) | copy-start | bytes 12292
  788.2 90.0 %copy-start.65 = (f32[128]{0:T(128)S(1)}, f32[128]{0:T(128)}, u32[]{:S(2)}) copy-start(f32[128]{0:T(128)} %copy-done.64) | copy-start | bytes 1540
  788.3 90.0 %copy-start.83 = (f32[128]{0:T(128)S(1)}, f32[128]{0:T(128)}, u32[]{:S(2)}) copy-start(f32[128]{0:T(128)} %copy-done.82) | copy-start | bytes 1540
  788.6 91.6 %copy-start.56 = (bf16[128,1024]{1,0:T(8,128)(2,1)}, bf16[128,1024]{1,0:T(8,128)(2,1)S(1)}, u32[]{:S(2)}) copy-start(bf16[128,1024]{1,0:T(8,128)(2,1)S(1)} %copy.213) | copy-start | bytes 786436
  802.3 77.9 %copy-start.31 = (bf16[128,2048]{1,0:T(8,128)(2,1)}, bf16[128,2048]{1,0:T(8,128)(2,1)S(1)}, u32[]{:S(2)}) copy-start(bf16[128,2048]{1,0:T(8,128)(2,1)S(1)} %convert.17) | copy-start | bytes 1572868
  886.7 667.4 %reduce-scatter.17.cloned.1.call-start = ((), (), s32[]{:S(2)}) async-start(), calls=%async_computation.18 | async-start | bytes 17301504 | tf_op jit(solution)/shard_map/reduce_scatter | solution.py:330
  900.3 1019.0 %reduce-scatter.15.cloned.1.call-start = ((), (), s32[]{:S(2)}) async-start(), calls=%async_computation.17 | async-start | bytes 17301504 | tf_op jit(solution)/shard_map/reduce_scatter | solution.py:328
  913.2 11.8 copy-start.78
  913.2 11.8 copy-start.79
  913.2 11.8 copy-start.72
  913.2 11.8 copy-start.73
  913.2 11.8 copy-start.70
  913.2 11.8 copy-start.71
  913.2 11.8 copy-start.76
  913.3 11.8 copy-start.77
  913.3 11.8 copy-start.74
  913.3 11.8 copy-start.75
  925.1 5.8 copy-start.23
  925.1 11.9 slice-start.2
  930.9 6.0 copy-start.32
  930.9 6.1 copy-start.38
  930.9 6.2 slice-start.3
  930.9 6.2 copy-start.40
  939.4 45.9 %copy-start.28 = (f32[128,1024]{1,0:T(8,128)S(1)}, f32[128,1024]{1,0:T(8,128)}, u32[]{:S(2)}) copy-start(f32[128,1024]{1,0:T(8,128)} %copy-done.26) | copy-start | bytes 1572868
  939.4 45.9 %copy-start.30 = (f32[128,1024]{1,0:T(8,128)S(1)}, f32[128,1024]{1,0:T(8,128)}, u32[]{:S(2)}) copy-start(f32[128,1024]{1,0:T(8,128)} %get-tuple-element.881) | copy-start | bytes 1572868
  (61 other events, 127.0 us)
Sparse Core Ops, SparseCore 0:
  9.6 118.0 all-gather.15
  132.5 26.1 all-gather.25
  160.6 27.8 all-gather.27
  190.3 27.8 all-gather.19
  219.9 27.8 all-gather.17
  249.3 98.9 all-gather.21
  349.9 206.7 all-gather.23
  732.3 68.6 reduce-scatter.8
  804.9 71.2 reduce-scatter.6
  878.9 148.1 reduce-scatter.12
  1033.6 154.2 reduce-scatter.10
  1190.7 363.3 reduce-scatter.16
  1557.0 362.1 reduce-scatter.14
